TPU v7x, 32 devices: a whole 2x2x4 slice. The times are simulated.
32 devices in a mesh: seq: 8 (over y, x, core), head: 4 (over z).
Axes of the slice: x: 2, y: 2, z: 4, core: 2. Of those that a mesh axis runs over, the one named last changes fastest.
Arguments:
- out_grad: bfloat16 [2048, 4096], P('seq', 'head'), may hold values from -7.2 to 7.2
- x_in: bfloat16 [2048, 4096], P('seq', 'head'), may hold values from -6 to 6
- b_in: bfloat16 [2048, 128], P('seq'), may hold values from -2.5 to 2.5
- c_in: bfloat16 [2048, 128], P('seq'), may hold values from -2.5 to 2.5
- dt_raw: float32 [64, 2048], P('head', 'seq'), may hold values from -5.1 to -0.7
- dt_bias: float32 [64], P('head'), may hold values from -0.5 to 0.5
- a_log: float32 [64], P('head'), may hold values from -7.5 to 2.2
- d_skip: float32 [64], P('head'), may hold values from 0.5 to 1.5
- states: bfloat16 [8, 4096, 128], P('seq', 'head'), may hold values from -6 to 6
- w_out: bfloat16 [4096, 4096], P('head'), may hold values from -0.09375 to 0.09375
- w_in: bfloat16 [4096, 4096], P(None, 'head'), may hold values from -0.125 to 0.125
Outputs:
- in_grad: bfloat16 [4096, 2048], P('head', 'seq')
- bc_grad: bfloat16 [256, 2048], P('head', 'seq')
- dt_grad: float32 [64, 2048], P('head', 'seq')
- param_grad: float32 [3, 64], P(None, 'head')
All inputs are finite; a program needn't handle non-finite values.
Results may differ from a plain program's by a relative error of at most 0.015.
Values may be sent and summed in bfloat16 or wider, within the bound.
A program may use at most 64 MiB of HBM per device.

v0:
```python
import jax
import jax.numpy as jnp
from jax import lax
from jax.sharding import PartitionSpec as P


def entering(value, axis, join, neutral):
    count, mine = (lax.axis_size(axis), lax.axis_index(axis))
    pieces = jax.tree.map(lambda part: lax.all_gather(part, axis), value)
    pieces = jax.tree.map(lambda part: part[::-1], pieces)
    mine = count - 1 - mine
    so_far = jax.tree.map(
        lambda part, zero: jnp.full_like(part, 0) + jnp.asarray(zero, part.dtype), value, neutral
    )

    def turn(position, so_far):
        longer = join(so_far, jax.tree.map(lambda part: part[position], pieces))
        return jax.tree.map(lambda new, old: jnp.where(position < mine, new, old), longer, so_far)

    return lax.fori_loop(0, count - 1, turn, so_far)


def shards(out_grad, x_in, b_in, c_in, dt_raw, dt_bias, a_log, d_skip, states, w_out, w_in):
    tokens_here, inner_here = x_in.shape
    group_heads = dt_raw.shape[0]
    head_dim = inner_here // group_heads
    state_dim = b_in.shape[1]
    contract_last = (((1,), (1,)), ((), ()))
    head_sum = lax.dot_general(
        lax.all_gather(out_grad, "head", axis=1, tiled=True),
        w_out,
        contract_last,
        preferred_element_type=jnp.float32,
    )
    dy_heads = head_sum.astype(jnp.bfloat16).reshape(tokens_here, group_heads, head_dim)
    dy_wide = dy_heads.astype(jnp.float32)
    x_heads = x_in.reshape(tokens_here, group_heads, head_dim)
    x_wide = x_heads.astype(jnp.float32)
    decay_rate = jnp.exp(a_log)
    step_size = jax.nn.softplus(dt_raw + dt_bias[:, None])
    log_step = -decay_rate[:, None] * step_size
    cumlog = jnp.cumsum(log_step, axis=1)
    positions = jnp.arange(tokens_here)
    causal = positions[:, None] >= positions[None, :]
    log_gaps = cumlog[:, :, None] - cumlog[:, None, :]
    decay_mask = jnp.where(causal[None], jnp.exp(jnp.minimum(log_gaps, 0.0)), 0.0)
    scores = lax.dot_general(c_in, b_in, contract_last, preferred_element_type=jnp.float32)
    step_rows = step_size.T
    x_scaled = (x_wide * step_rows[:, :, None]).astype(jnp.bfloat16)
    pair_dots = jnp.einsum("ihp,jhp->hij", dy_heads, x_scaled, preferred_element_type=jnp.float32)
    kernel = (scores[None] * decay_mask).astype(jnp.bfloat16)
    intra_back = jnp.einsum("hij,ihp->jhp", kernel, dy_heads, preferred_element_type=jnp.float32)
    masked_dots = (pair_dots * decay_mask).astype(jnp.bfloat16)
    start_decay = jnp.exp(cumlog)
    dy_decay = (dy_wide * start_decay.T[:, :, None]).astype(jnp.bfloat16)
    local_state = jnp.einsum("ihp,in->hpn", dy_decay, c_in, preferred_element_type=jnp.float32)
    end_total = jnp.exp(cumlog[:, -1])
    entry_state = states.reshape(group_heads, head_dim, state_dim)
    db_intra = jnp.einsum("hij,in->nj", masked_dots, c_in, preferred_element_type=jnp.float32)
    dc_intra = jnp.einsum("hij,jn->ni", masked_dots, b_in, preferred_element_type=jnp.float32)
    dc_entry = jnp.einsum("ihp,hpn->ni", dy_decay, entry_state, preferred_element_type=jnp.float32)
    ystate = jnp.einsum("in,hpn->ihp", c_in, entry_state, preferred_element_type=jnp.float32)
    pair_weight = pair_dots * scores[None] * decay_mask
    state_terms = start_decay * jnp.sum(dy_wide * ystate, axis=2).T
    skip_terms = jnp.sum(dy_wide * x_wide, axis=(0, 2))

    def compose(earlier, nearer):
        return (nearer[0] * earlier[0], nearer[0][:, None, None] * earlier[1] + nearer[1])

    identity_pair = (jnp.ones_like(end_total), jnp.zeros_like(local_state))
    carried = entering((end_total, local_state), "seq", compose, identity_pair)[1]
    carried_bf = carried.astype(jnp.bfloat16)
    state_back = jnp.einsum("jn,hpn->jhp", b_in, carried_bf, preferred_element_type=jnp.float32)
    end_decay = jnp.exp(cumlog[:, -1:] - cumlog)
    end_weight = (step_size * end_decay).T
    x_grad = (
        (
            step_rows[:, :, None] * intra_back
            + end_weight[:, :, None] * state_back
            + d_skip[None, :, None] * dy_wide
        )
        .astype(jnp.bfloat16)
        .reshape(tokens_here, inner_here)
    )
    x_end = (x_wide * end_weight[:, :, None]).astype(jnp.bfloat16)
    db_entry = jnp.einsum("jhp,hpn->nj", x_end, carried_bf, preferred_element_type=jnp.float32)
    bc_part = jnp.concatenate([db_intra + db_entry, dc_intra + dc_entry], axis=0)
    end_terms = end_weight.T * jnp.sum(x_wide * state_back, axis=2).T
    cum_grad = pair_weight.sum(axis=2) - pair_weight.sum(axis=1) + state_terms - end_terms
    tail_grad = end_terms.sum(axis=1) + end_total * jnp.sum(
        entry_state.astype(jnp.float32) * carried, axis=(1, 2)
    )
    cum_grad = cum_grad.at[:, -1].add(tail_grad)
    step_grad = jnp.cumsum(cum_grad[:, ::-1], axis=1)[:, ::-1]
    dt_sum = (
        -decay_rate[:, None] * step_grad
        + jnp.sum(x_wide * (intra_back + end_decay.T[:, :, None] * state_back), axis=2).T
    )
    dt_grad = dt_sum * jax.nn.sigmoid(dt_raw + dt_bias[:, None])
    param_terms = jnp.stack(
        [jnp.sum(step_grad * log_step, axis=1), skip_terms, jnp.sum(dt_grad, axis=1)]
    )
    in_part = lax.psum_scatter(
        lax.dot_general(w_in, x_grad, contract_last, preferred_element_type=jnp.float32).astype(
            jnp.bfloat16
        ),
        "head",
        scatter_dimension=0,
        tiled=True,
    )
    bc_sum = lax.psum_scatter(bc_part.astype(jnp.bfloat16), "head", scatter_dimension=0, tiled=True)
    norm_scale = (lax.axis_size("seq") * tokens_here * head_dim) ** (-0.5)
    param_grad = lax.psum(param_terms, "seq") * norm_scale
    return (in_part, bc_sum, dt_grad, param_grad)


def solution(mesh):
    return jax.shard_map(
        shards,
        mesh=mesh,
        in_specs=(
            P("seq", "head"),
            P("seq", "head"),
            P("seq", None),
            P("seq", None),
            P("head", "seq"),
            P("head"),
            P("head"),
            P("head"),
            P("seq", "head", None),
            P("head", None),
            P(None, "head"),
        ),
        out_specs=(P("head", "seq"), P("head", "seq"), P("head", "seq"), P(None, "head")),
        check_vma=False,
    )
```

profile of v0, /device:TPU:0, one launch (start us, length us, event | category | flops | bytes accessed | tf_op | source)
XLA Modules:
  0.0 200.9 jit_solution(2288571976925971934)
XLA Ops:
  9.2 0.8 copy_bitcast_fusion.3
  11.0 1.4 fusion.35
  12.9 45.1 %all-gather.5.cloned.1.call-done = bf16[256,4096]{1,0:T(8,128)(2,1)} async-done(((bf16[256,1024]{1,0:T(8,128)(2,1)}), bf16[256,4096]{1,0:T(8,128)(2,1)}) %all-gather.5.cloned.1.call-update) | async-done | bytes 2097168 | tf_op jit(solution)/shard_map/all_gather | solution.py:30
  58.0 7.8 %fusion.17 = (f32[1024]{0:T(1024)}, bf16[256,1024]{1,0:T(8,128)(2,1)}, bf16[256,1024]{1,0:T(8,128)(2,1)S(1)}) fusion(bf16[256,1024]{1,0:T(8,128)(2,1)} %param.16, f32[256,1024]{1,0:T(8,128)S(1)} %copy.72, bf16[256,4096]{1,0:T(8,128)(2,1)} %all-gather.5.cloned.1.call-done, bf16[1024,4096]{1,0:T(8,128)(2,1)} %param.24), kind=kOutput, calls=%fused_computation.36 | convolution fusion | flops 2149317632 | bytes 13111296 | tf_op jit(solution)/shard_map/dot_general | solution.py:29
  66.0 1.1 fusion.22
  68.9 13.9 %all-reduce = f32[128]{0:T(128)S(1)} all-reduce(f32[128]{0:T(128)S(1)} %dynamic-update-slice.3), channel_id=2, replica_groups=mesh['seq'=8,'head'=4] {'seq'}, use_global_device_ids=true, to_apply=%add | all-reduce | flops 128 | bytes 1024
  84.1 2.0 fusion.10
  86.1 16.6 %all-gather.7.cloned.1.call-done = f32[128,64,128]{2,1,0:T(8,128)} async-done(((f32[16,64,128]{2,1,0:T(8,128)}), f32[128,64,128]{2,1,0:T(8,128)}) %all-gather.7.cloned.1.call-update) | async-done | bytes 4194320 | tf_op jit(solution)/shard_map/all_gather | solution.py:9
  102.8 4.7 %rev.13 = f32[8,16,64,128]{3,2,1,0:T(8,128)} reverse(f32[8,16,64,128]{3,2,1,0:T(8,128)} %bitcast.136), dimensions={0} | reverse | bytes 8388608 | tf_op jit(solution)/shard_map/rev | solution.py:10
  107.5 13.2 %while.15 = (s32[]{:T(128)}, f32[16,64,128]{2,1,0:T(8,128)S(1)}, s32[]{:T(128)}, f32[8,16]{1,0:T(8,128)}, f32[8,16,64,128]{3,2,1,0:T(8,128)}, /*index=5*/s32[]{:T(128)}, s32[]{:T(128)}) while((s32[]{:T(128)}, f32[16,64,128]{2,1,0:T(8,128)S(1)}, s32[]{:T(128)}, f32[8,16]{1,0:T(8,128)}, f32[8,16,64,128]{3,2,1,0:T(8,128)}, ...), condition=%wide.region_3.4_spmd.clone, body=%wide.region_2.3_spmd.clone.sunk | while | flops 524292 | bytes 1573161 | solution.py:20
  108.2 1.2 fusion.62
  110.1 1.2 fusion.62
  112.0 1.2 fusion.62
  113.9 1.2 fusion.62
  115.7 1.2 fusion.62
  117.6 1.2 fusion.62
  119.5 1.2 fusion.62
  120.7 1.2 multiply_reduce_fusion.1
  121.9 7.2 %fusion.1 = bf16[4096,256]{0,1:T(8,128)(2,1)} fusion(bf16[256,1024]{0,1:T(8,128)(2,1)S(1)} %bitcast.142, bf16[4096,1024]{1,0:T(8,128)(2,1)} %param.25), kind=kOutput, calls=%fused_computation.4 | convolution fusion | flops 2148532224 | bytes 11010048 | tf_op jit(solution)/shard_map/dot_general | solution.py:104
  131.0 3.5 %fusion.2 = (f32[16,256]{1,0:T(8,128)S(1)}, f32[16,256]{1,0:T(8,128)S(1)}, bf16[256,256]{1,0:T(8,128)(2,1)S(1)}) fusion(f32[16,256]{1,0:T(8,128)} %copy-done.13, f32[256,256]{1,0:T(8,128)} %copy-done.5, pred[256,256]{1,0:T(8,128)(4,1)} %copy-done.15, bf16[256,16,64]{0,2,1:T(8,128)(2,1)S(1)} %bitcast.135, f32[256,16,64]{0,2,1:T(8,128)S(1)} %bitcast.130, ...), kind=kOutput, calls=%fused_computation.10 | convolution fusion | flops 146202624 | bytes 2097152 | tf_op jit(solution)/shard_map/ihp,jhp->hij/dot_general | solution.py:50
  138.7 13.9 %psum.7 = f32[3,16]{1,0:T(4,128)S(1)} all-reduce(f32[3,16]{1,0:T(4,128)S(1)} %pad_maximum_fusion.1), channel_id=1, replica_groups=mesh['seq'=8,'head'=4] {'seq'}, use_global_device_ids=true, to_apply=%region_20.21 | all-reduce | flops 48 | bytes 384 | tf_op jit(solution)/shard_map/psum | solution.py:113
  153.2 19.8 %reduce-scatter.3.cloned.1.call-done = bf16[1024,256]{0,1:T(8,128)(2,1)} async-done(((bf16[4096,256]{0,1:T(8,128)(2,1)}), bf16[1024,256]{0,1:T(8,128)(2,1)}) %reduce-scatter.3.cloned.1.call-update) | async-done | bytes 524304 | tf_op jit(solution)/shard_map/reduce_scatter | solution.py:103
  173.0 2.0 %copy.78 = bf16[1024,256]{1,0:T(8,128)(2,1)} copy(bf16[1024,256]{0,1:T(8,128)(2,1)} %reduce-scatter.3.cloned.1.call-done) | data formatting | bytes 1048576
  175.0 19.4 %reduce-scatter.5.cloned.1.call-done = bf16[64,256]{1,0:T(8,128)(2,1)} async-done(((bf16[256,256]{1,0:T(8,128)(2,1)}), bf16[64,256]{1,0:T(8,128)(2,1)}) %reduce-scatter.5.cloned.1.call-update) | async-done | bytes 32784 | tf_op jit(solution)/shard_map/reduce_scatter | solution.py:111
  (114 shorter events, 17.3 us)
Async XLA Ops:
  7.2 76.3 %copy-start = (bf16[256,128]{1,0:T(8,128)(2,1)S(1)}, bf16[256,128]{1,0:T(8,128)(2,1)}, u32[]{:S(2)}) copy-start(bf16[256,128]{1,0:T(8,128)(2,1)} %param.17) | copy-start | bytes 196612
  7.2 50.8 %all-gather.5.cloned.1.call-start = ((), (), s32[]{:S(2)}) async-start(), calls=%async_computation.2 | async-start | bytes 2621440 | tf_op jit(solution)/shard_map/all_gather | solution.py:30
  7.9 94.9 %all-gather.7.cloned.1.call-start = ((), (), s32[]{:S(2)}) async-start(), calls=%async_computation.5 | async-start | bytes 4718592 | tf_op jit(solution)/shard_map/all_gather | solution.py:9
  10.8 55.0 %copy-start.16 = (f32[16,2]{0,1:T(2,128)}, f32[16,2]{0,1:T(2,128)S(1)}, u32[]{:S(2)}) copy-start(f32[16,2]{0,1:T(2,128)S(1)} %slice.34) | copy-start | bytes 388
  11.0 54.8 %copy-start.19 = (f32[16]{0:T(128)}, f32[16]{0:T(128)S(1)}, u32[]{:S(2)}) copy-start(f32[16]{0:T(128)S(1)} %get-tuple-element.154) | copy-start | bytes 196
  12.9 53.1 %copy-start.2 = (bf16[256,128]{1,0:T(8,128)(2,1)S(1)}, bf16[256,128]{1,0:T(8,128)(2,1)}, u32[]{:S(2)}) copy-start(bf16[256,128]{1,0:T(8,128)(2,1)} %param.18) | copy-start | bytes 196612
  12.9 54.3 %copy-start.3 = (bf16[256,1024]{1,0:T(8,128)(2,1)S(1)}, bf16[256,1024]{1,0:T(8,128)(2,1)}, u32[]{:S(2)}) copy-start(bf16[256,1024]{1,0:T(8,128)(2,1)} %param.16) | copy-start | bytes 1572868
  67.2 105.8 %reduce-scatter.3.cloned.1.call-start = ((), (), s32[]{:S(2)}) async-start(), calls=%async_computation.3 | async-start | bytes 2621440 | tf_op jit(solution)/shard_map/reduce_scatter | solution.py:103
  84.1 23.4 %copy-start.5 = (f32[256,256]{1,0:T(8,128)}, f32[256,256]{1,0:T(8,128)S(1)}, u32[]{:S(2)}) copy-start(f32[256,256]{1,0:T(8,128)S(1)} %fusion.44) | copy-start | bytes 786436
  107.5 13.2 %copy-start.7 = (f32[256,16]{0,1:T(8,128)S(1)}, f32[256,16]{0,1:T(8,128)}, u32[]{:S(2)}) copy-start(f32[256,16]{0,1:T(8,128)} %get-tuple-element.175) | copy-start | bytes 49156
  107.5 13.2 %copy-start.9 = (f32[256,16]{0,1:T(8,128)S(1)}, f32[256,16]{0,1:T(8,128)}, u32[]{:S(2)}) copy-start(f32[256,16]{0,1:T(8,128)} %get-tuple-element.176) | copy-start | bytes 49156
  107.5 13.2 %copy-start.10 = (f32[256,16]{0,1:T(8,128)S(1)}, f32[256,16]{0,1:T(8,128)}, u32[]{:S(2)}) copy-start(f32[256,16]{0,1:T(8,128)} %get-tuple-element.174) | copy-start | bytes 49156
  107.5 13.2 %copy-start.25 = (f32[16]{0:T(128)S(1)}, f32[16]{0:T(128)}, u32[]{:S(2)}) copy-start(f32[16]{0:T(128)} %param.22) | copy-start | bytes 196
  121.9 7.3 %copy-start.21 = (f32[1024]{0:T(1024)S(1)}, f32[1024]{0:T(1024)}, u32[]{:S(2)}) copy-start(f32[1024]{0:T(1024)} %get-tuple-element.169) | copy-start | bytes 12292
  121.9 8.1 %copy-start.4 = (bf16[256,1024]{1,0:T(8,128)(2,1)S(1)}, bf16[256,1024]{1,0:T(8,128)(2,1)}, u32[]{:S(2)}) copy-start(bf16[256,1024]{1,0:T(8,128)(2,1)} %get-tuple-element.170) | copy-start | bytes 1572868
  121.9 8.3 %copy-start.1 = (bf16[1,1024,128]{2,1,0:T(8,128)(2,1)S(1)}, bf16[1,1024,128]{2,1,0:T(8,128)(2,1)}, u32[]{:S(2)}) copy-start(bf16[1,1024,128]{2,1,0:T(8,128)(2,1)} %param.23) | copy-start | bytes 786436
  129.2 65.2 %reduce-scatter.5.cloned.1.call-start = ((), (), s32[]{:S(2)}) async-start(), calls=%async_computation.4 | async-start | bytes 163840 | tf_op jit(solution)/shard_map/reduce_scatter | solution.py:111
  130.8 3.8 %copy-start.6 = (f32[16,256]{1,0:T(8,128)S(1)}, f32[16,256]{1,0:T(8,128)}, u32[]{:S(2)}) copy-start(f32[16,256]{1,0:T(8,128)} %param.19) | copy-start | bytes 49156
  130.9 3.8 %copy-start.11 = (f32[256,16]{0,1:T(8,128)S(1)}, f32[256,16]{0,1:T(8,128)}, u32[]{:S(2)}) copy-start(f32[256,16]{0,1:T(8,128)} %get-tuple-element.152) | copy-start | bytes 49156
  130.9 4.4 %copy-start.14 = (f32[16,256]{1,0:T(8,128)S(1)}, f32[16,256]{1,0:T(8,128)}, u32[]{:S(2)}) copy-start(f32[16,256]{1,0:T(8,128)} %copy-done.13) | copy-start | bytes 49156
  130.9 5.8 %copy-start.8 = (f32[256,16]{0,1:T(8,128)S(1)}, f32[256,16]{0,1:T(8,128)}, u32[]{:S(2)}) copy-start(f32[256,16]{0,1:T(8,128)} %get-tuple-element.175) | copy-start | bytes 49156
  130.9 6.9 %copy-start.12 = (f32[256,16]{0,1:T(8,128)S(1)}, f32[256,16]{0,1:T(8,128)}, u32[]{:S(2)}) copy-start(f32[256,16]{0,1:T(8,128)} %get-tuple-element.153) | copy-start | bytes 49156
  130.9 6.9 %copy-start.23 = (f32[16]{0:T(128)S(1)}, f32[16]{0:T(128)}, u32[]{:S(2)}) copy-start(f32[16]{0:T(128)} %copy-done.22) | copy-start | bytes 196
  130.9 7.7 %copy-start.24 = (f32[16]{0:T(128)S(1)}, f32[16]{0:T(128)}, u32[]{:S(2)}) copy-start(f32[16]{0:T(128)} %reduce_sum.127) | copy-start | bytes 196
  (7 other events, 15.9 us)
Sparse Core Ops, SparseCore 0:
  9.6 48.3 all-gather.4
  67.3 35.4 all-gather.6
  129.3 43.6 reduce-scatter.2
  175.7 18.6 reduce-scatter.4
where the time goes:
time: 202 us; the launch traced here: 201 us
  waiting for transfers between devices  102 us (50%)
  blocking collectives  27.8 us (14%)
  matrix products  24.4 us (12%)
  local copies, waits for them, and re-layouts  16.4 us (8%)
  other arithmetic  15.7 us (8%)
  between operations  14.7 us (7%)
    all_gather x1, waiting for transfers between devices, shards(): lax.all_gather(out_grad, 'head', axis=1, tiled=True)  45.1 us
    reduce_scatter x1, waiting for transfers between devices, shards(): lax.psum_scatter(lax.dot_general(w_in, x_grad, contract_last, preferred_e...  19.8 us
    reduce_scatter x1, waiting for transfers between devices, shards(): lax.psum_scatter(bc_part.astype(jnp.bfloat16), 'head', scatter_dimension=...  19.4 us
    all_gather x1, waiting for transfers between devices, entering(): pieces = jax.tree.map(lambda part: lax.all_gather(part, axis), value)  16.6 us
    unnamed x1, blocking collectives  13.9 us
    psum x1, blocking collectives, shards(): param_grad = lax.psum(param_terms, 'seq') * norm_scale  13.9 us
    select_n x7, other arithmetic, turn(): jnp.where(position < mine, new, old)  8.18 us
    dot_general x1, matrix products, shards(): lax.dot_general(lax.all_gather(out_grad, 'head', axis=1, tiled=True), w_o...  7.83 us
  transfers between devices with their start and end apart: 4, of which 4 were waited for; matrix products, arithmetic and copies ran while one was open for 10% of the time, Pallas kernels for 0%

commit v1 on v0

--- a/solution.py
+++ b/solution.py
@@ -2,6 +2,21 @@
 import jax.numpy as jnp
 from jax import lax
 from jax.sharding import PartitionSpec as P
+
+
+def end_links_for(work_x):
+    along_axis = "head"
+    devs = jax.lax.psum(1, along_axis)
+    samples = [(rr, (rr + 1) % devs) for rr in range(devs)]
+    blocks_here = [(rr, (rr - 1) % devs) for rr in range(devs)]
+    field_out, reached = ([work_x], [work_x])
+    for _ in range(devs // 2):
+        field_out.append(jax.lax.ppermute(field_out[-1], along_axis, samples))
+    for _ in range((devs - 1) // 2):
+        reached.append(jax.lax.ppermute(reached[-1], along_axis, blocks_here))
+    later = jnp.concatenate([*field_out[::-1], *reached[1:]], 1)
+    then = jnp.roll(later, (jax.lax.axis_index(along_axis) - devs // 2) * work_x.shape[1], axis=1)
+    return then
 
 
 def entering(value, axis, join, neutral):
@@ -27,10 +42,7 @@
     state_dim = b_in.shape[1]
     contract_last = (((1,), (1,)), ((), ()))
     head_sum = lax.dot_general(
-        lax.all_gather(out_grad, "head", axis=1, tiled=True),
-        w_out,
-        contract_last,
-        preferred_element_type=jnp.float32,
+        end_links_for(out_grad), w_out, contract_last, preferred_element_type=jnp.float32
     )
     dy_heads = head_sum.astype(jnp.bfloat16).reshape(tokens_here, group_heads, head_dim)
     dy_wide = dy_heads.astype(jnp.float32)

time: 202 us -> 192 us (0.950)
  waiting for transfers between devices: 102 us -> 87.1 us
  starting transfers between devices: 0.16 us -> 5.5 us
    all_gather x1 -> x0, waiting for transfers between devices: 45.1 us -> none  [shards(): lax.all_gather(out_grad, 'head', axis=1, tiled=True)]
    ppermute x0 -> x3, waiting for transfers between devices: none -> 29.2 us  [the longest x2 29.2 us: end_links_for(): field_out.append(jax.lax.ppermute(field_out[-1], along_axis, samples))]
    ppermute x0 -> x3, starting transfers between devices: none -> 5.2 us  [the longest x2 3.11 us: end_links_for(): field_out.append(jax.lax.ppermute(field_out[-1], along_axis, samples))]
    all_gather x1, waiting for transfers between devices: 16.6 us -> 18.8 us  [entering(): pieces = jax.tree.map(lambda part: lax.all_gather(part, axis), value)]
  transfers between devices with their start and end apart: 4 -> 6, of which waited for: 4 -> 5; matrix products, arithmetic and copies ran while one was open for 10% -> 11% of each run, Pallas kernels for 0% -> 0%
where the time goes in v1:
time: 192 us; the launch traced here: 190 us
  waiting for transfers between devices  87.1 us (45%)
  blocking collectives  26.2 us (14%)
  matrix products  23.8 us (12%)
  local copies, waits for them, and re-layouts  17.1 us (9%)
  other arithmetic  15.7 us (8%)
  between operations  14.8 us (8%)
  starting transfers between devices  5.5 us (3%)
    ppermute x2, waiting for transfers between devices, end_links_for(): field_out.append(jax.lax.ppermute(field_out[-1], along_axis, samples))  29.2 us
    reduce_scatter x1, waiting for transfers between devices, shards(): lax.psum_scatter(lax.dot_general(w_in, x_grad, contract_last, preferred_e...  19.7 us
    reduce_scatter x1, waiting for transfers between devices, shards(): lax.psum_scatter(bc_part.astype(jnp.bfloat16), 'head', scatter_dimension=...  19.5 us
    all_gather x1, waiting for transfers between devices, entering(): pieces = jax.tree.map(lambda part: lax.all_gather(part, axis), value)  18.8 us
    psum x1, blocking collectives, shards(): param_grad = lax.psum(param_terms, 'seq') * norm_scale  13.9 us
    unnamed x1, blocking collectives  12.3 us
    select_n x7, other arithmetic, turn(): jnp.where(position < mine, new, old)  8.18 us
    dot_general x1, matrix products, shards(): lax.dot_general(end_links_for(out_grad), w_out, contract_last, preferred_...  7.29 us
  transfers between devices with their start and end apart: 6, of which 5 were waited for; matrix products, arithmetic and copies ran while one was open for 11% of the time, Pallas kernels for 0%

profile of v1, /device:TPU:0, one launch (start us, length us, event | category | flops | bytes accessed | tf_op | source)
XLA Modules:
  0.0 190.5 jit_solution(15319737084740426277)
XLA Ops:
  7.2 3.1 %collective-permute-start = (bf16[256,1024]{1,0:T(8,128)(2,1)}, bf16[256,1024]{1,0:T(8,128)(2,1)S(1)}, u32[]{:S(2)}, u32[]{:S(2)}) collective-permute-start(bf16[256,1024]{1,0:T(8,128)(2,1)} %param.15), channel_id=1, source_target_pairs={{0,1},{1,2},{2,3},{3,0},{4,5},{5,6},{6,7},{7,4},{8,9},{9,10},{10,1... | collective-permute-start | bytes 1572872 | tf_op jit(solution)/shard_map/ppermute | solution.py:14
  10.3 2.1 %collective-permute-start.2 = (bf16[256,1024]{1,0:T(8,128)(2,1)}, bf16[256,1024]{1,0:T(8,128)(2,1)S(1)}, u32[]{:S(2)}, u32[]{:S(2)}) collective-permute-start(bf16[256,1024]{1,0:T(8,128)(2,1)} %param.15), channel_id=1, source_target_pairs={{0,3},{1,0},{2,1},{3,2},{4,7},{5,4},{6,5},{7,6},{8,11},{9,8},{10,9... | collective-permute-start | bytes 1572872 | tf_op jit(solution)/shard_map/ppermute | solution.py:16
  14.7 10.7 %collective-permute-done = bf16[256,1024]{1,0:T(8,128)(2,1)S(1)} collective-permute-done((bf16[256,1024]{1,0:T(8,128)(2,1)}, bf16[256,1024]{1,0:T(8,128)(2,1)S(1)}, u32[]{:S(2)}, u32[]{:S(2)}) %collective-permute-start) | collective-permute-done | bytes 524320 | tf_op jit(solution)/shard_map/ppermute | solution.py:14
  25.7 1.4 fusion.40
  27.2 1.3 copy.72
  28.5 18.5 %collective-permute-done.1 = bf16[256,1024]{1,0:T(8,128)(2,1)S(1)} collective-permute-done((bf16[256,1024]{1,0:T(8,128)(2,1)S(1)}, bf16[256,1024]{1,0:T(8,128)(2,1)S(1)}, u32[]{:S(2)}, u32[]{:S(2)}) %collective-permute-start.1) | collective-permute-done | bytes 524320 | tf_op jit(solution)/shard_map/ppermute | solution.py:14
  47.5 7.3 %fusion.22 = (f32[1024]{0:T(1024)}, bf16[256,1024]{1,0:T(8,128)(2,1)}, bf16[256,1024]{1,0:T(8,128)(2,1)S(1)}) fusion(bf16[256,1024]{1,0:T(8,128)(2,1)S(1)} %copy-done.5, f32[256,1024]{1,0:T(8,128)S(1)} %copy-done.2, bf16[1024,4096]{1,0:T(8,128)(2,1)} %param.24, bf16[256,8192]{1,0:T(8,128)(2,1)S(1)} %constant_dynamic-update-slice_fusion, s32[]{:T(128)S(6)} %select_n.45), kind=kOutput, calls=%fused_computation.38 | convolution fusion | flops 2149317632 | bytes 13111300 | tf_op jit(solution)/shard_map/dot_general | solution.py:44
  57.8 12.3 %all-reduce = f32[128]{0:T(128)S(1)} all-reduce(f32[128]{0:T(128)S(1)} %dynamic-update-slice.3), channel_id=2, replica_groups=mesh['seq'=8,'head'=4] {'seq'}, use_global_device_ids=true, to_apply=%add | all-reduce | flops 128 | bytes 1024
  71.4 2.0 %fusion.12 = f32[256,16,64]{0,2,1:T(8,128)S(1)} fusion(bf16[256,16,64]{0,2,1:T(8,128)(2,1)S(1)} %bitcast.132, f32[16,256]{1,0:T(8,128)} %copy-done.16, f32[256,256]{1,0:T(8,128)S(1)} %fusion.50, pred[256,256]{1,0:T(8,128)(4,1)S(1)} %iota_compare_fusion), kind=kOutput, calls=%fused_computation.23 | convolution fusion | flops 139460608 | bytes 1916928 | tf_op jit(solution)/shard_map/hij,ihp->jhp/dot_general | solution.py:64
  73.4 18.8 %all-gather.4.cloned.1.call-done = f32[128,64,128]{2,1,0:T(8,128)} async-done(((f32[16,64,128]{2,1,0:T(8,128)}), f32[128,64,128]{2,1,0:T(8,128)}) %all-gather.4.cloned.1.call-update) | async-done | bytes 4194320 | tf_op jit(solution)/shard_map/all_gather | solution.py:24
  92.2 4.7 %rev.13 = f32[8,16,64,128]{3,2,1,0:T(8,128)} reverse(f32[8,16,64,128]{3,2,1,0:T(8,128)} %bitcast.135), dimensions={0} | reverse | bytes 8388608 | tf_op jit(solution)/shard_map/rev | solution.py:25
  96.9 13.2 %while.15 = (s32[]{:T(128)}, f32[16,64,128]{2,1,0:T(8,128)S(1)}, s32[]{:T(128)}, f32[8,16]{1,0:T(8,128)}, f32[8,16,64,128]{3,2,1,0:T(8,128)}, /*index=5*/s32[]{:T(128)}, s32[]{:T(128)}) while((s32[]{:T(128)}, f32[16,64,128]{2,1,0:T(8,128)S(1)}, s32[]{:T(128)}, f32[8,16]{1,0:T(8,128)}, f32[8,16,64,128]{3,2,1,0:T(8,128)}, ...), condition=%wide.region_3.4_spmd.clone, body=%wide.region_2.3_spmd.clone.sunk | while | flops 524292 | bytes 1573161 | solution.py:35
  97.7 1.2 fusion.67
  99.5 1.2 fusion.67
  101.4 1.2 fusion.67
  103.3 1.2 fusion.67
  105.2 1.2 fusion.67
  110.1 1.2 multiply_reduce_fusion.1
  111.4 7.2 %fusion.1 = bf16[4096,256]{0,1:T(8,128)(2,1)} fusion(bf16[256,1024]{0,1:T(8,128)(2,1)S(1)} %bitcast.141, bf16[4096,1024]{1,0:T(8,128)(2,1)} %param.25), kind=kOutput, calls=%fused_computation.4 | convolution fusion | flops 2148532224 | bytes 11010048 | tf_op jit(solution)/shard_map/dot_general | solution.py:116
  120.6 3.5 %fusion.2 = (f32[16,256]{1,0:T(8,128)S(1)}, f32[16,256]{1,0:T(8,128)S(1)}, bf16[256,256]{1,0:T(8,128)(2,1)S(1)}) fusion(f32[16,256]{1,0:T(8,128)} %copy-done.16, f32[256,256]{1,0:T(8,128)} %copy-done.8, pred[256,256]{1,0:T(8,128)(4,1)} %copy-done.18, bf16[256,16,64]{0,2,1:T(8,128)(2,1)S(1)} %bitcast.134, f32[256,16,64]{0,2,1:T(8,128)S(1)} %bitcast.129, ...), kind=kOutput, calls=%fused_computation.10 | convolution fusion | flops 146202624 | bytes 2097152 | tf_op jit(solution)/shard_map/ihp,jhp->hij/dot_general | solution.py:62
  128.3 13.9 %psum.7 = f32[3,16]{1,0:T(4,128)S(1)} all-reduce(f32[3,16]{1,0:T(4,128)S(1)} %pad_maximum_fusion.1), channel_id=1, replica_groups=mesh['seq'=8,'head'=4] {'seq'}, use_global_device_ids=true, to_apply=%region_20.21 | all-reduce | flops 48 | bytes 384 | tf_op jit(solution)/shard_map/psum | solution.py:125
  142.8 19.7 %reduce-scatter.3.cloned.1.call-done = bf16[1024,256]{0,1:T(8,128)(2,1)} async-done(((bf16[4096,256]{0,1:T(8,128)(2,1)}), bf16[1024,256]{0,1:T(8,128)(2,1)}) %reduce-scatter.3.cloned.1.call-update) | async-done | bytes 524304 | tf_op jit(solution)/shard_map/reduce_scatter | solution.py:115
  162.4 2.0 %copy.78 = bf16[1024,256]{1,0:T(8,128)(2,1)} copy(bf16[1024,256]{0,1:T(8,128)(2,1)} %reduce-scatter.3.cloned.1.call-done) | data formatting | bytes 1048576
  164.5 19.5 %reduce-scatter.5.cloned.1.call-done = bf16[64,256]{1,0:T(8,128)(2,1)} async-done(((bf16[256,256]{1,0:T(8,128)(2,1)}), bf16[64,256]{1,0:T(8,128)(2,1)}) %reduce-scatter.5.cloned.1.call-update) | async-done | bytes 32784 | tf_op jit(solution)/shard_map/reduce_scatter | solution.py:123
  (131 shorter events, 20.4 us)
Async XLA Ops:
  7.2 63.6 %copy-start = (bf16[256,128]{1,0:T(8,128)(2,1)S(1)}, bf16[256,128]{1,0:T(8,128)(2,1)}, u32[]{:S(2)}) copy-start(bf16[256,128]{1,0:T(8,128)(2,1)} %param.17) | copy-start | bytes 196612
  7.2 39.9 %copy-start.1 = (bf16[256,1024]{1,0:T(8,128)(2,1)S(1)}, bf16[256,1024]{1,0:T(8,128)(2,1)}, u32[]{:S(2)}) copy-start(bf16[256,1024]{1,0:T(8,128)(2,1)} %param.15) | copy-start | bytes 1572868
  7.2 85.0 %all-gather.4.cloned.1.call-start = ((), (), s32[]{:S(2)}) async-start(), calls=%async_computation.4 | async-start | bytes 4718592 | tf_op jit(solution)/shard_map/all_gather | solution.py:24
  7.2 18.2 %collective-permute-start = (bf16[256,1024]{1,0:T(8,128)(2,1)}, bf16[256,1024]{1,0:T(8,128)(2,1)S(1)}, u32[]{:S(2)}, u32[]{:S(2)}) collective-permute-start(bf16[256,1024]{1,0:T(8,128)(2,1)} %param.15), channel_id=1, source_target_pairs={{0,1},{1,2},{2,3},{3,0},{4,5},{5,6},{6,7},{7,4},{8,9},{9,10},{10,1... | collective-permute-start | bytes 1572872 | tf_op jit(solution)/shard_map/ppermute | solution.py:14
  10.3 36.8 %collective-permute-start.2 = (bf16[256,1024]{1,0:T(8,128)(2,1)}, bf16[256,1024]{1,0:T(8,128)(2,1)S(1)}, u32[]{:S(2)}, u32[]{:S(2)}) collective-permute-start(bf16[256,1024]{1,0:T(8,128)(2,1)} %param.15), channel_id=1, source_target_pairs={{0,3},{1,0},{2,1},{3,2},{4,7},{5,4},{6,5},{7,6},{8,11},{9,8},{10,9... | collective-permute-start | bytes 1572872 | tf_op jit(solution)/shard_map/ppermute | solution.py:16
  14.7 32.6 %copy-start.19 = (f32[16,2]{0,1:T(2,128)}, f32[16,2]{0,1:T(2,128)S(1)}, u32[]{:S(2)}) copy-start(f32[16,2]{0,1:T(2,128)S(1)} %slice.34) | copy-start | bytes 388
  25.4 21.6 %collective-permute-start.1 = (bf16[256,1024]{1,0:T(8,128)(2,1)S(1)}, bf16[256,1024]{1,0:T(8,128)(2,1)S(1)}, u32[]{:S(2)}, u32[]{:S(2)}) collective-permute-start(bf16[256,1024]{1,0:T(8,128)(2,1)S(1)} %collective-permute-done), channel_id=1, source_target_pairs={{0,1},{1,2},{2,3},{3,0},{4,5},{5,6},{6,7},{7,4},{8,9},{9,10},{10,1... | collective-permute-start | bytes 1572872 | tf_op jit(solution)/shard_map/ppermute | solution.py:14
  25.5 21.8 %copy-start.16 = (f32[16,256]{1,0:T(8,128)}, f32[16,256]{1,0:T(8,128)S(1)}, u32[]{:S(2)}) copy-start(f32[16,256]{1,0:T(8,128)S(1)} %copy_bitcast_fusion.1) | copy-start | bytes 49156
  25.7 21.6 %copy-start.22 = (f32[16]{0:T(128)}, f32[16]{0:T(128)S(1)}, u32[]{:S(2)}) copy-start(f32[16]{0:T(128)S(1)} %get-tuple-element.154) | copy-start | bytes 196
  28.5 18.9 %copy-start.2 = (f32[256,1024]{1,0:T(8,128)S(1)}, f32[256,1024]{1,0:T(8,128)}, u32[]{:S(2)}) copy-start(f32[256,1024]{1,0:T(8,128)} %copy.72) | copy-start | bytes 3145732
  28.5 18.9 %copy-start.5 = (bf16[256,1024]{1,0:T(8,128)(2,1)S(1)}, bf16[256,1024]{1,0:T(8,128)(2,1)}, u32[]{:S(2)}) copy-start(bf16[256,1024]{1,0:T(8,128)(2,1)} %param.16) | copy-start | bytes 1572868
  47.4 7.5 %copy-start.4 = (bf16[256,128]{1,0:T(8,128)(2,1)S(1)}, bf16[256,128]{1,0:T(8,128)(2,1)}, u32[]{:S(2)}) copy-start(bf16[256,128]{1,0:T(8,128)(2,1)} %param.18) | copy-start | bytes 196612
  47.5 8.7 %copy-start.6 = (bf16[256,1024]{1,0:T(8,128)(2,1)S(1)}, bf16[256,1024]{1,0:T(8,128)(2,1)}, u32[]{:S(2)}) copy-start(bf16[256,1024]{1,0:T(8,128)(2,1)} %param.16) | copy-start | bytes 1572868
  56.1 106.3 %reduce-scatter.3.cloned.1.call-start = ((), (), s32[]{:S(2)}) async-start(), calls=%async_computation.2 | async-start | bytes 2621440 | tf_op jit(solution)/shard_map/reduce_scatter | solution.py:115
  71.4 25.5 %copy-start.8 = (f32[256,256]{1,0:T(8,128)}, f32[256,256]{1,0:T(8,128)S(1)}, u32[]{:S(2)}) copy-start(f32[256,256]{1,0:T(8,128)S(1)} %fusion.50) | copy-start | bytes 786436
  96.9 13.2 %copy-start.10 = (f32[256,16]{0,1:T(8,128)S(1)}, f32[256,16]{0,1:T(8,128)}, u32[]{:S(2)}) copy-start(f32[256,16]{0,1:T(8,128)} %get-tuple-element.175) | copy-start | bytes 49156
  96.9 13.2 %copy-start.12 = (f32[256,16]{0,1:T(8,128)S(1)}, f32[256,16]{0,1:T(8,128)}, u32[]{:S(2)}) copy-start(f32[256,16]{0,1:T(8,128)} %get-tuple-element.176) | copy-start | bytes 49156
  96.9 13.2 %copy-start.13 = (f32[256,16]{0,1:T(8,128)S(1)}, f32[256,16]{0,1:T(8,128)}, u32[]{:S(2)}) copy-start(f32[256,16]{0,1:T(8,128)} %get-tuple-element.174) | copy-start | bytes 49156
  96.9 13.2 %copy-start.28 = (f32[16]{0:T(128)S(1)}, f32[16]{0:T(128)}, u32[]{:S(2)}) copy-start(f32[16]{0:T(128)} %param.22) | copy-start | bytes 196
  111.4 7.5 %copy-start.24 = (f32[1024]{0:T(1024)S(1)}, f32[1024]{0:T(1024)}, u32[]{:S(2)}) copy-start(f32[1024]{0:T(1024)} %get-tuple-element.169) | copy-start | bytes 12292
  111.4 8.3 %copy-start.7 = (bf16[256,1024]{1,0:T(8,128)(2,1)S(1)}, bf16[256,1024]{1,0:T(8,128)(2,1)}, u32[]{:S(2)}) copy-start(bf16[256,1024]{1,0:T(8,128)(2,1)} %get-tuple-element.170) | copy-start | bytes 1572868
  111.4 8.5 %copy-start.3 = (bf16[1,1024,128]{2,1,0:T(8,128)(2,1)S(1)}, bf16[1,1024,128]{2,1,0:T(8,128)(2,1)}, u32[]{:S(2)}) copy-start(bf16[1,1024,128]{2,1,0:T(8,128)(2,1)} %param.23) | copy-start | bytes 786436
  118.6 65.3 %reduce-scatter.5.cloned.1.call-start = ((), (), s32[]{:S(2)}) async-start(), calls=%async_computation.3 | async-start | bytes 163840 | tf_op jit(solution)/shard_map/reduce_scatter | solution.py:123
  120.6 7.7 %copy-start.27 = (f32[16]{0:T(128)S(1)}, f32[16]{0:T(128)}, u32[]{:S(2)}) copy-start(f32[16]{0:T(128)} %reduce_sum.127) | copy-start | bytes 196
  (12 other events, 47.0 us)
Sparse Core Ops, SparseCore 0:
  56.2 35.9 all-gather.3
  118.8 43.6 reduce-scatter.2
  165.3 18.6 reduce-scatter.4
